TPU v7x, 256 devices: a whole 4x4x8 slice. The times are simulated.
256 devices in a mesh: cx: 8 (over z), cy: 32 (over y, x, core).
Axes of the slice: x: 4, y: 4, z: 8, core: 2. Of those that a mesh axis runs over, the one named last changes fastest.
Arguments:
- points_block: bfloat16 [2048, 64, 256], P(('cx', 'cy')), may hold values from -6 to 6
- leaf_basis: bfloat16 [2048, 64, 256], P(('cx', 'cy')), may hold values from -0.375 to 0.375
- near_blocks: bfloat16 [2048, 4, 256, 256], P(('cx', 'cy')), may hold values from -0.1875 to 0.1875
- near_ids: int32 [2048, 4], P(('cx', 'cy')), may hold values from 0 to 2047, as said below
- local_transfer: bfloat16 [1792, 128, 64], P(('cx', 'cy')), may hold values from -0.5 to 0.5
- far_coupling: bfloat16 [2048, 8, 64, 64], P(('cx', 'cy')), may hold values from -0.25 to 0.25
- far_ids: int32 [2048, 8], P(('cx', 'cy')), may hold values from 0 to 2047, as said below
- upper_transfer: bfloat16 [255, 128, 64], replicated, may hold values from -0.5 to 0.5
- upper_coupling: bfloat16 [255, 64, 64], replicated, may hold values from -0.75 to 0.75
Outputs:
- product: bfloat16 [2048, 64, 256], P(('cx', 'cy'))
Inputs may be any that keep to these rules, and one draw needn't show every extreme that they name: `near_ids`: slot 0 of each leaf is the leaf itself; every id names a leaf of the same device or of the two devices before or after it, devices numbered in the order cx then cy. `far_ids`: every id names a leaf of the same device or of the two devices before or after it, devices numbered in the order cx then cy.
All inputs are finite; a program needn't handle non-finite values.
Results may differ from a plain program's by a relative error of at most 0.004.
Values may be sent and summed in bfloat16 or wider, within the bound.
No kernel may reach another device: no remote copies, remote signals or barrier semaphores. Data moves between devices by JAX's collectives and lax.ppermute only.
A program may use at most 128 MiB of HBM per device.

v0:
```python
import jax
import jax.numpy as jnp
from jax import lax
from jax.experimental import pallas as pl
from jax.experimental.pallas import tpu as pltpu
from jax.sharding import PartitionSpec as P

F32 = jnp.float32
BF16 = jnp.bfloat16
AXES = ("cx", "cy")
VM = pl.BlockSpec(memory_space=pltpu.VMEM)
SM = pl.BlockSpec(memory_space=pltpu.SMEM)
HB = pl.BlockSpec(memory_space=pltpu.HBM)
ANY = pl.BlockSpec(memory_space=pl.ANY)
HBM = pltpu.HBM
VMEM = pltpu.VMEM


def position():
    return lax.axis_index("cx") * lax.axis_size("cy") + lax.axis_index("cy")


def mm(a, b):
    return lax.dot_general(a, b, (((1,), (0,)), ((), ())), preferred_element_type=F32)


def mt(a, b):
    return lax.dot_general(a, b, (((1,), (1,)), ((), ())), preferred_element_type=F32)


def high_low(x):
    high = x.astype(BF16)
    return high, (x - high.astype(F32)).astype(BF16)


def split(x):
    return jnp.concatenate(high_low(x), axis=0)


def fold(y):
    half = y.shape[0] // 2
    return y[:half] + y[half:]


def up(left, right, transfer):
    return fold(mt(jnp.concatenate([left, right], axis=1), transfer))


def packed(x):
    return jnp.concatenate([x[:32], x[32:]], axis=1)


def unpacked(x):
    return jnp.concatenate([x[:, :64], x[:, 64:]], axis=0)


def leaf_up_kernel(
    points, basis, local, transfer, halo, root_out, first_out, plane_out, basis_here, local_here, sems
):
    pos = position()
    plane = pos >> 5
    copies = [
        (points, halo.at[pl.ds(0, 8)]), (basis, basis_here), (local, local_here),
        (transfer.at[pos >> 1], first_out),
    ]
    base = 128
    at = 0
    for count in (8, 4, 2, 1):
        copies.append((transfer.at[pl.ds(base + plane * count, count)], plane_out.at[pl.ds(at, count)]))
        base += count * 8
        at += count
    handles = [pltpu.make_async_copy(a, b, sems.at[i]) for i, (a, b) in enumerate(copies)]
    for handle in handles:
        handle.start()
    for handle in handles[:2]:
        handle.wait()
    skel = [mt(halo[g], basis_here[g]) for g in range(8)]
    handles[2].wait()
    for half in range(2):
        halo[8 + half] = jnp.concatenate(skel[4 * half : 4 * half + 4], axis=1).astype(BF16)
    offset = 0
    while len(skel) > 1:
        parts = [split(x) for x in skel]
        skel = [
            up(parts[2 * n], parts[2 * n + 1], local_here[offset + n])
            for n in range(len(parts) // 2)
        ]
        offset += len(skel)
    root_out[...] = packed(skel[0])
    for handle in handles[3:]:
        handle.wait()


def merge_kernel(root, partner, transfer, message, sibling):
    odd = position() & 1
    own = unpacked(root[...])
    other = unpacked(partner[...])
    sibling[...] = other
    left = split(jnp.where(odd == 1, other, own))
    right = split(jnp.where(odd == 1, own, other))
    merged = packed(up(left, right, transfer[...]))
    for peer in range(16):
        message[peer] = merged


def assemble_kernel(halo, partner, pair, sems):
    odd = position() & 1
    handles = [
        pltpu.make_async_copy(halo, pair.at[odd], sems.at[0]),
        pltpu.make_async_copy(partner, pair.at[1 - odd], sems.at[1]),
    ]
    for handle in handles:
        handle.start()
    for handle in handles:
        handle.wait()


def halves_of(x):
    return x[:, :64], x[:, 64:]


def weights_kernel(
    transfer, coupling_in, local_in, basis, blocks, far_coupling,
    top_out, down_high, down_low, leaf_high, leaf_low, basis_out, blocks_out, far_coupling_out,
    own_transfer, own_coupling, coupling, local, sems,
):
    pos = position()
    copies = [(coupling_in, coupling), (local_in, local)]
    base = 0
    for level in range(1, 9):
        copies.append((transfer.at[base + (pos >> level)], own_transfer.at[level - 1]))
        base += 256 >> level
    early = len(copies)
    copies += [
        (transfer.at[pl.ds(248, 6)], top_out), (far_coupling, far_coupling_out),
        (basis, basis_out), (blocks, blocks_out),
    ]
    handles = [pltpu.make_async_copy(a, b, sems.at[i]) for i, (a, b) in enumerate(copies)]
    for handle in handles:
        handle.start()
    for handle in handles[:early]:
        handle.wait()
    level_of_row = lax.broadcasted_iota(jnp.int32, (8, 255), 0) + 1
    wanted = 256 - (512 >> level_of_row) + (pos >> level_of_row)
    pick = jnp.where(lax.broadcasted_iota(jnp.int32, (8, 255), 1) == wanted, 1.0, 0.0).astype(BF16)
    for row in range(64):
        own_coupling[row] = mt(pick, coupling[row])
    tops = list(halves_of(local[6].astype(F32)))
    for first, count in ((4, 2), (0, 4)):
        products = []
        for n in range(count):
            products.append(fold(mm(split(tops[n]), local[first + n])))
        if first:
            tops = [half for x in products for half in halves_of(x)]
    for n in range(4):
        leaf_high[n], leaf_low[n] = high_low(products[n])
    row = lax.broadcasted_iota(jnp.int32, (64, 64), 0)
    col = lax.broadcasted_iota(jnp.int32, (64, 64), 1)
    path = jnp.where(row == col, 1.0, 0.0).astype(F32)
    for level in range(1, 9):
        side = (pos >> (level - 1)) & 1
        both = split(path)
        block = own_coupling[:, level - 1, :].astype(BF16)
        term = jnp.where(side == 0, fold(mm(both, block)), fold(mt(both, block)))
        down_high[level - 1], down_low[level - 1] = high_low(term)
        if level < 8:
            left, right = halves_of(own_transfer[level - 1])
            path = fold(mt(both, jnp.where(side == 0, left, right)))
    for handle in handles[early:]:
        handle.wait()


def sweep(first, transfer, nodes, levels):
    parts = first
    offset = 0
    at = 0
    for _ in range(levels):
        count = len(parts) // 2
        halves = [split(x) for x in parts]
        parts = [
            up(halves[2 * n], halves[2 * n + 1], transfer[offset + n]) for n in range(count)
        ]
        offset += count
        at += 2 * count
        for n in range(count):
            nodes[at + n] = parts[n]
    return parts


def plane_kernel(received, transfer, message, siblings, nodes):
    first = [unpacked(received[n]) for n in range(16)]
    for n in range(16):
        nodes[n] = first[n]
    top = sweep(first, transfer, nodes, 4)
    root = packed(top[0])
    for peer in range(8):
        message[peer] = root
    own = (position() >> 1) & 15
    at = 0
    for level in range(4):
        siblings[level] = nodes[at + ((own >> level) ^ 1)]
        at += 16 >> level


def add_terms(total, siblings, down_high, down_low, first):
    for n, sibling in enumerate(siblings):
        both = split(sibling)
        total = total + fold(mt(both, down_high[first + n])) + mt(both[:64], down_low[first + n])
    return total


def near_far_kernel(
    near_ids, far_ids, pair, moved, passed, blocks, coupling, sibling, siblings,
    down_high, down_low, near_out, far_out, coef_out, skels,
):
    pos = position()
    odd = pos & 1
    pair_at, moved_at, passed_at = 2 - odd, 3 * odd, 4 - 4 * odd
    coef_out[...] = add_terms(
        jnp.zeros((64, 64), F32), [sibling[...]] + [siblings[n] for n in range(4)],
        down_high, down_low, 0,
    )
    first_leaf = (pos - 2) * 8
    for source, at, count in ((pair, pair_at, 2), (moved, moved_at, 2), (passed, passed_at, 1)):
        for device in range(count):
            for leaf in range(8):
                lane = 64 * (leaf % 4)
                skels[8 * (at + device) + leaf] = source[device, 8 + leaf // 4, :, lane : lane + 64]
    for g in range(8):
        total = mt(pair[odd, g], blocks[g, 0])
        for k in range(1, 4):
            place = jnp.clip(near_ids[k, g] - first_leaf, 0, 39)
            device, leaf = place >> 3, place & 7
            from_pair, from_moved = device - pair_at, device - moved_at
            cols = jnp.where(
                (from_pair >> 1) == 0, pair[from_pair & 1, leaf],
                jnp.where(
                    (from_moved >> 1) == 0, moved[from_moved & 1, leaf], passed[0, leaf]
                ),
            )
            total = total + mt(cols, blocks[g, k])
        near_out[g] = total
        total = None
        for k in range(8):
            place = jnp.clip(far_ids[g, k] - first_leaf, 0, 39)
            term = mt(skels[place], coupling[g, k])
            total = term if total is None else total + term
        far_out[g] = total


def final_kernel(
    received, transfer, down_high, down_low, leaf_high, leaf_low, coef, near, far, basis, out, nodes,
):
    first = [unpacked(received[n]) for n in range(8)]
    for n in range(8):
        nodes[n] = first[n]
    sweep(first, transfer, nodes, 2)
    own = position() >> 5
    siblings = []
    at = 0
    for level in range(3):
        siblings.append(nodes[at + ((own >> level) ^ 1)])
        at += 8 >> level
    total = add_terms(coef[...], siblings, down_high, down_low, 5)
    both = split(total)
    for pair in range(4):
        coefs = fold(mm(both, leaf_high[pair])) + mm(both[:64], leaf_low[pair])
        for side, part in enumerate(halves_of(coefs)):
            g = 2 * pair + side
            half = (part + far[g]).astype(BF16)
            out[g] = (mm(half, basis[g]) + near[g]).astype(BF16)


def call(kernel, ins, outs, in_specs, scratch=(), limit=4, out_spec=VM):
    ins = [
        pltpu.with_memory_space_constraint(x, pltpu.HBM) if spec is HB else x
        for x, spec in zip(ins, in_specs)
    ]
    return pl.pallas_call(
        kernel,
        out_shape=[space(shape, dtype) for shape, dtype, space in outs],
        in_specs=in_specs,
        out_specs=[out_spec] * len(outs),
        scratch_shapes=list(scratch),
        compiler_params=pltpu.CompilerParams(vmem_limit_bytes=limit << 20),
    )(*ins)


def groups_of(bits):
    mask = sum(1 << b for b in bits)
    found = {}
    for device in range(256):
        found.setdefault(device & ~mask, []).append(device)
    return list(found.values())


def exchange(message, bits):
    return lax.all_to_all(message, AXES, 0, 0, axis_index_groups=groups_of(bits))


def swapped(value):
    return lax.ppermute(value, AXES, [(i, i ^ 1) for i in range(lax.axis_size(AXES))])


def outward(value):
    count = lax.axis_size(AXES)
    pairs = [(i, i + 2 - 4 * (i % 2)) for i in range(count)]
    return lax.ppermute(value, AXES, [(i, j) for i, j in pairs if 0 <= j < count])


def local(
    points, basis, near_blocks, near_ids, local_transfer, far_coupling, far_ids,
    upper_transfer, upper_coupling,
):
    near_ids = near_ids.T
    local_transfer = jnp.swapaxes(local_transfer, 1, 2)
    upper_transfer = jnp.swapaxes(upper_transfer, 1, 2)
    upper_coupling = jnp.transpose(upper_coupling, (1, 2, 0))
    halo, root, first, plane = call(
        leaf_up_kernel, (points, basis, local_transfer, upper_transfer),
        [
            ((10, 64, 256), BF16, HBM), ((32, 128), F32, VMEM), ((64, 128), BF16, VMEM),
            ((15, 64, 128), BF16, VMEM),
        ],
        [HB] * 4,
        [pltpu.VMEM((8, 64, 256), BF16), pltpu.VMEM((7, 64, 128), BF16), pltpu.SemaphoreType.DMA((8,))],
    )
    partner = swapped(root)
    partner_halo = swapped(halo)
    message, sibling = call(
        merge_kernel, (root, partner, first),
        [((16, 32, 128), F32, HBM), ((64, 64), F32, VMEM)], [VM] * 3,
    )
    received = exchange(message, (1, 2, 3, 4))
    (pair,) = call(
        assemble_kernel, (halo, partner_halo), [((2, 10, 64, 256), BF16, VMEM)],
        [HB, ANY], [pltpu.SemaphoreType.DMA((2,))],
    )
    moved = outward(pair)
    message, siblings = call(
        plane_kernel, (received, plane),
        [((8, 32, 128), F32, HBM), ((4, 64, 64), F32, VMEM)], [VM] * 2,
        [pltpu.VMEM((31, 64, 64), F32)],
    )
    received = exchange(message, (5, 6, 7))
    odd = lax.axis_index("cy") & 1
    passed = swapped(lax.dynamic_slice_in_dim(moved, 1 - odd, 1, 0))
    top, down_high, down_low, leaf_high, leaf_low, basis, near_blocks, far_coupling = call(
        weights_kernel,
        (upper_transfer, upper_coupling, local_transfer, basis, near_blocks, far_coupling),
        [((6, 64, 128), BF16, VMEM)] + [((8, 64, 64), BF16, VMEM)] * 2
        + [((4, 64, 128), BF16, VMEM)] * 2
        + [((8, 64, 256), BF16, VMEM), ((8, 4, 256, 256), BF16, VMEM), ((8, 8, 64, 64), BF16, VMEM)],
        [HB] * 6,
        [
            pltpu.VMEM((8, 64, 128), BF16), pltpu.VMEM((64, 8, 64), F32),
            pltpu.VMEM((64, 64, 255), BF16), pltpu.VMEM((7, 64, 128), BF16),
            pltpu.SemaphoreType.DMA((14,)),
        ],
        limit=8,
    )
    near, far, coef = call(
        near_far_kernel,
        (near_ids, far_ids, pair, moved, passed, near_blocks, far_coupling, sibling, siblings,
         down_high, down_low),
        [((8, 64, 256), F32, VMEM), ((8, 64, 64), F32, VMEM), ((64, 64), F32, VMEM)],
        [SM, SM] + [VM] * 9,
        [pltpu.VMEM((40, 64, 64), BF16)],
    )
    (out,) = call(
        final_kernel,
        (received, top, down_high, down_low, leaf_high, leaf_low, coef, near, far, basis),
        [((8, 64, 256), BF16, HBM)], [VM] * 10,
        [pltpu.VMEM((14, 64, 64), F32)],
    )
    return out


def solution(mesh):
    return jax.shard_map(
        local,
        mesh=mesh,
        in_specs=(
            P(AXES, None, None),
            P(AXES, None, None),
            P(AXES, None, None, None),
            P(AXES, None),
            P(AXES, None, None),
            P(AXES, None, None, None),
            P(AXES, None),
            P(),
            P(),
        ),
        out_specs=P(AXES, None, None),
        check_vma=False,
    )
```

profile of v0, /device:TPU:1, one launch (start us, length us, event | category | flops | bytes accessed | tf_op | source)
XLA Modules:
  0.0 48.0 jit_solution(6250382348974255548)
XLA Ops:
  0.0 2.7 %shard_map.91 = (bf16[10,64,256]{2,1,0:T(8,128)(2,1)}, f32[32,128]{1,0:T(8,128)S(1)}, bf16[64,128]{1,0:T(8,128)(2,1)S(1)}, bf16[15,64,128]{2,1,0:T(8,128)(2,1)S(1)}) custom-call(bf16[8,64,256]{2,1,0:T(8,128)(2,1)} %points.1, bf16[8,64,256]{2,1,0:T(8,128)(2,1)} %basis.3, bf16[7,64,128]{2,1,0:T(8,128)(2,1)} %bitcast.8, bf16[255,64,128]{2,1,0:T(8,128)(2,1)} %bitcast.5), custom_call_target="tpu_custom_call" | custom-call | tf_op jit(solution)/shard_map/pallas_call | solution.py:279
  2.7 3.3 %collective-permute-start.1 = (bf16[10,64,256]{2,1,0:T(8,128)(2,1)}, bf16[10,64,256]{2,1,0:T(8,128)(2,1)S(1)}, u32[]{:S(2)}, u32[]{:S(2)}) collective-permute-start(bf16[10,64,256]{2,1,0:T(8,128)(2,1)} %get-tuple-element.34.halo), channel_id=1, source_target_pairs={{0,1},{1,0},{2,3},{3,2},{4,5},{5,4},{6,7},{7,6},{8,9},{9,8},{10,11... | collective-permute-start | bytes 983048 | tf_op jit(solution)/shard_map/ppermute | solution.py:302
  6.0 1.5 %collective-permute-done.1.partner = bf16[10,64,256]{2,1,0:T(8,128)(2,1)S(1)} collective-permute-done((bf16[10,64,256]{2,1,0:T(8,128)(2,1)}, bf16[10,64,256]{2,1,0:T(8,128)(2,1)S(1)}, u32[]{:S(2)}, u32[]{:S(2)}) %collective-permute-start.1) | collective-permute-done | bytes 327712 | tf_op jit(solution)/shard_map/ppermute | solution.py:302
  7.5 1.0 %shard_map.95.pair = bf16[2,10,64,256]{3,2,1,0:T(8,128)(2,1)S(1)} custom-call(bf16[10,64,256]{2,1,0:T(8,128)(2,1)} %get-tuple-element.34.halo, bf16[10,64,256]{2,1,0:T(8,128)(2,1)S(1)} %collective-permute-done.1.partner), custom_call_target="tpu_custom_call" | custom-call | tf_op jit(solution)/shard_map/pallas_call | solution.py:279
  8.5 1.3 %collective-permute-start.2 = (bf16[2,10,64,256]{3,2,1,0:T(8,128)(2,1)S(1)}, bf16[2,10,64,256]{3,2,1,0:T(8,128)(2,1)S(1)}, u32[]{:S(2)}, u32[]{:S(2)}) collective-permute-start(bf16[2,10,64,256]{3,2,1,0:T(8,128)(2,1)S(1)} %shard_map.95.pair), channel_id=1, source_target_pairs={{0,2},{2,4},{3,1},{4,6},{5,3},{6,8},{7,5},{8,10},{9,7},{10,12},{11... | collective-permute-start | bytes 1966088 | tf_op jit(solution)/shard_map/ppermute | solution.py:308
  9.8 0.9 %collective-permute-start = (f32[32,128]{1,0:T(8,128)S(1)}, f32[32,128]{1,0:T(8,128)S(1)}, u32[]{:S(2)}, u32[]{:S(2)}) collective-permute-start(f32[32,128]{1,0:T(8,128)S(1)} %get-tuple-element.24.root), channel_id=1, source_target_pairs={{0,1},{1,0},{2,3},{3,2},{4,5},{5,4},{6,7},{7,6},{8,9},{9,8},{10,11... | collective-permute-start | bytes 49160 | tf_op jit(solution)/shard_map/ppermute | solution.py:302
  10.7 0.8 %collective-permute-done.partner = f32[32,128]{1,0:T(8,128)S(1)} collective-permute-done((f32[32,128]{1,0:T(8,128)S(1)}, f32[32,128]{1,0:T(8,128)S(1)}, u32[]{:S(2)}, u32[]{:S(2)}) %collective-permute-start) | collective-permute-done | bytes 16416 | tf_op jit(solution)/shard_map/ppermute | solution.py:302
  11.5 1.1 %shard_map.92 = (f32[16,32,128]{2,1,0:T(8,128)}, f32[64,64]{1,0:T(8,128)S(1)}) custom-call(f32[32,128]{1,0:T(8,128)S(1)} %get-tuple-element.24.root, f32[32,128]{1,0:T(8,128)S(1)} %collective-permute-done.partner, bf16[64,128]{1,0:T(8,128)(2,1)S(1)} %get-tuple-element.25.transfer), custom_call_target="tpu_custom_call" | custom-call | tf_op jit(solution)/shard_map/pallas_call | solution.py:279
  12.6 6.4 %all-to-all-start = ((f32[16,32,128]{2,1,0:T(8,128)}), f32[16,32,128]{2,1,0:T(8,128)S(1)}, u32[]{:S(2)}, u32[]{:S(2)}) async-start(f32[16,32,128]{2,1,0:T(8,128)} %get-tuple-element.26), calls=%async_computation | async-start | bytes 524288 | tf_op jit(solution)/shard_map/all_to_all | solution.py:298
  19.0 0.8 %collective-permute-done.2.moved = bf16[2,10,64,256]{3,2,1,0:T(8,128)(2,1)S(1)} collective-permute-done((bf16[2,10,64,256]{3,2,1,0:T(8,128)(2,1)S(1)}, bf16[2,10,64,256]{3,2,1,0:T(8,128)(2,1)S(1)}, u32[]{:S(2)}, u32[]{:S(2)}) %collective-permute-start.2) | collective-permute-done | bytes 655392 | tf_op jit(solution)/shard_map/ppermute | solution.py:308
  19.8 0.7 %constant_dynamic-slice_fusion = bf16[1,10,64,256]{3,2,1,0:T(8,128)(2,1)} fusion(bf16[2,10,64,256]{3,2,1,0:T(8,128)(2,1)S(1)} %collective-permute-done.2.moved, s32[]{:T(128)S(6)} %select_n.3), kind=kLoop, calls=%fused_computation | loop fusion | bytes 655364 | tf_op jit(solution)/shard_map/dynamic_slice | solution.py:347
  20.6 0.0 collective-permute-start.3
  20.6 6.6 %all-to-all-done.received = f32[16,32,128]{2,1,0:T(8,128)S(1)} async-done(((f32[16,32,128]{2,1,0:T(8,128)}), f32[16,32,128]{2,1,0:T(8,128)S(1)}, u32[]{:S(2)}, u32[]{:S(2)}) %all-to-all-start) | async-done | bytes 262176 | tf_op jit(solution)/shard_map/all_to_all | solution.py:298
  27.2 1.6 %shard_map.93 = (f32[8,32,128]{2,1,0:T(8,128)}, f32[4,64,64]{2,1,0:T(8,128)S(1)}) custom-call(f32[16,32,128]{2,1,0:T(8,128)S(1)} %all-to-all-done.received, bf16[15,64,128]{2,1,0:T(8,128)(2,1)S(1)} %get-tuple-element.27.transfer), custom_call_target="tpu_custom_call" | custom-call | tf_op jit(solution)/shard_map/pallas_call | solution.py:279
  28.8 9.0 %all-to-all-start.1 = ((f32[8,32,128]{2,1,0:T(8,128)}), f32[8,32,128]{2,1,0:T(8,128)S(1)}, u32[]{:S(2)}, u32[]{:S(2)}) async-start(f32[8,32,128]{2,1,0:T(8,128)} %get-tuple-element.28), calls=%async_computation.1 | async-start | bytes 262144 | tf_op jit(solution)/shard_map/all_to_all | solution.py:298
  37.8 0.0 copy-start
  37.8 0.0 copy-start.1
  37.8 4.1 %shard_map.94 = (bf16[6,64,128]{2,1,0:T(8,128)(2,1)S(1)}, bf16[8,64,64]{2,1,0:T(8,128)(2,1)S(1)}, bf16[8,64,64]{2,1,0:T(8,128)(2,1)S(1)}, bf16[4,64,128]{2,1,0:T...) custom-call(bf16[255,64,128]{2,1,0:T(8,128)(2,1)} %bitcast.6, ...), custom_call_target="tpu_custom_call" | custom-call | tf_op jit(solution)/shard_map/pallas_call | solution.py:279
  41.9 0.0 collective-permute-done.3.passed
  41.9 0.0 copy-done
  41.9 0.0 copy-done.1
  41.9 2.6 %shard_map.96 = (f32[8,64,256]{2,1,0:T(8,128)S(1)}, f32[8,64,64]{2,1,0:T(8,128)S(1)}, f32[64,64]{1,0:T(8,128)S(1)}) custom-call(s32[4,8]{1,0:T(4,128)S(1)} %bitcast.4, s32[8,8]{1,0:T(8,128)S(1)} %copy-done, bf16[2,10,64,256]{3,2,1,0:T(8,128)(2,1)S(1)} %shard_map.95.pair, bf16[2,10,64,256]{3,2,1,0:T(8,128)(2,1)S(1)} %collective-permute-done.2.moved, ...), custom_call_target="tpu_custom_call" | custom-call | tf_op jit(solution)/shard_map/pallas_call | solution.py:279
  44.5 1.3 %all-to-all-done.1.received = f32[8,32,128]{2,1,0:T(8,128)S(1)} async-done(((f32[8,32,128]{2,1,0:T(8,128)}), f32[8,32,128]{2,1,0:T(8,128)S(1)}, u32[]{:S(2)}, u32[]{:S(2)}) %all-to-all-start.1) | async-done | bytes 131104 | tf_op jit(solution)/shard_map/all_to_all | solution.py:298
  45.8 2.1 %shard_map.97 = bf16[8,64,256]{2,1,0:T(8,128)(2,1)} custom-call(f32[8,32,128]{2,1,0:T(8,128)S(1)} %all-to-all-done.1.received, bf16[6,64,128]{2,1,0:T(8,128)(2,1)S(1)} %get-tuple-element.29.transfer, bf16[8,64,64]{2,1,0:T(8,128)(2,1)S(1)} %get-tuple-element.30.down_high, bf16[8,64,64]{2,1,0:T(8,128)(2,1)S(1)} %get-tuple-element.31.down_low, ...), custom_call_target="tpu_custom_call" | custom-call | tf_op jit(solution)/shard_map/pallas_call | solution.py:279
Async XLA Ops:
  2.7 4.8 %collective-permute-start.1 = (bf16[10,64,256]{2,1,0:T(8,128)(2,1)}, bf16[10,64,256]{2,1,0:T(8,128)(2,1)S(1)}, u32[]{:S(2)}, u32[]{:S(2)}) collective-permute-start(bf16[10,64,256]{2,1,0:T(8,128)(2,1)} %get-tuple-element.34.halo), channel_id=1, source_target_pairs={{0,1},{1,0},{2,3},{3,2},{4,5},{5,4},{6,7},{7,6},{8,9},{9,8},{10,11... | collective-permute-start | bytes 983048 | tf_op jit(solution)/shard_map/ppermute | solution.py:302
  8.5 11.3 %collective-permute-start.2 = (bf16[2,10,64,256]{3,2,1,0:T(8,128)(2,1)S(1)}, bf16[2,10,64,256]{3,2,1,0:T(8,128)(2,1)S(1)}, u32[]{:S(2)}, u32[]{:S(2)}) collective-permute-start(bf16[2,10,64,256]{3,2,1,0:T(8,128)(2,1)S(1)} %shard_map.95.pair), channel_id=1, source_target_pairs={{0,2},{2,4},{3,1},{4,6},{5,3},{6,8},{7,5},{8,10},{9,7},{10,12},{11... | collective-permute-start | bytes 1966088 | tf_op jit(solution)/shard_map/ppermute | solution.py:308
  9.8 1.7 %collective-permute-start = (f32[32,128]{1,0:T(8,128)S(1)}, f32[32,128]{1,0:T(8,128)S(1)}, u32[]{:S(2)}, u32[]{:S(2)}) collective-permute-start(f32[32,128]{1,0:T(8,128)S(1)} %get-tuple-element.24.root), channel_id=1, source_target_pairs={{0,1},{1,0},{2,3},{3,2},{4,5},{5,4},{6,7},{7,6},{8,9},{9,8},{10,11... | collective-permute-start | bytes 49160 | tf_op jit(solution)/shard_map/ppermute | solution.py:302
  12.6 14.6 %all-to-all-start = ((f32[16,32,128]{2,1,0:T(8,128)}), f32[16,32,128]{2,1,0:T(8,128)S(1)}, u32[]{:S(2)}, u32[]{:S(2)}) async-start(f32[16,32,128]{2,1,0:T(8,128)} %get-tuple-element.26), calls=%async_computation | async-start | bytes 524288 | tf_op jit(solution)/shard_map/all_to_all | solution.py:298
  20.6 21.4 %collective-permute-start.3 = (bf16[1,10,64,256]{3,2,1,0:T(8,128)(2,1)}, bf16[1,10,64,256]{3,2,1,0:T(8,128)(2,1)S(1)}, u32[]{:S(2)}, u32[]{:S(2)}) collective-permute-start(bf16[1,10,64,256]{3,2,1,0:T(8,128)(2,1)} %constant_dynamic-slice_fusion), channel_id=1, source_target_pairs={{0,1},{1,0},{2,3},{3,2},{4,5},{5,4},{6,7},{7,6},{8,9},{9,8},{10,11... | collective-permute-start | bytes 983048 | tf_op jit(solution)/shard_map/ppermute | solution.py:302
  28.8 17.0 %all-to-all-start.1 = ((f32[8,32,128]{2,1,0:T(8,128)}), f32[8,32,128]{2,1,0:T(8,128)S(1)}, u32[]{:S(2)}, u32[]{:S(2)}) async-start(f32[8,32,128]{2,1,0:T(8,128)} %get-tuple-element.28), calls=%async_computation.1 | async-start | bytes 262144 | tf_op jit(solution)/shard_map/all_to_all | solution.py:298
  37.8 4.1 %copy-start = (s32[8,8]{1,0:T(8,128)S(1)}, s32[8,8]{1,0:T(8,128)}, u32[]{:S(2)}) copy-start(s32[8,8]{1,0:T(8,128)} %far_ids.1) | copy-start | bytes 772
  37.8 4.1 %copy-start.1 = (s32[8,4]{0,1:T(4,128)S(1)}, s32[8,4]{0,1:T(4,128)}, u32[]{:S(2)}) copy-start(s32[8,4]{0,1:T(4,128)} %param.12) | copy-start | bytes 388
where the time goes:
time: 48.4 us; the launch traced here: 48 us
  starting transfers between devices  20.9 us (43%)
  Pallas kernels  15.2 us (31%)
  waiting for transfers between devices  11 us (23%)
  local copies, waits for them, and re-layouts  0.76 us (2%)
    all_to_all x2, starting transfers between devices, exchange(): lax.all_to_all(message, AXES, 0, 0, axis_index_groups=groups_of(bits))  15.4 us
    pallas_call x7, Pallas kernels, call(): pl.pallas_call(kernel, out_shape=[space(shape, dtype) for shape, dtype, s...  15.2 us
    all_to_all x2, waiting for transfers between devices, exchange(): lax.all_to_all(message, AXES, 0, 0, axis_index_groups=groups_of(bits))  7.92 us
    ppermute x3, starting transfers between devices, swapped(): lax.ppermute(value, AXES, [(i, i ^ 1) for i in range(lax.axis_size(AXES))])  4.18 us
    ppermute x3, waiting for transfers between devices, swapped(): lax.ppermute(value, AXES, [(i, i ^ 1) for i in range(lax.axis_size(AXES))])  2.31 us
    ppermute x1, starting transfers between devices, outward(): lax.ppermute(value, AXES, [(i, j) for i, j in pairs if 0 <= j < count])  1.29 us
  transfers between devices with their start and end apart: 6, of which 5 were waited for; matrix products, arithmetic and copies ran while one was open for 2% of the time, Pallas kernels for 19%

commit v1 on v0

--- a/solution.py
+++ b/solution.py
@@ -42,8 +42,12 @@
     return y[:half] + y[half:]
 
 
-def up(left, right, transfer):
-    return fold(mt(jnp.concatenate([left, right], axis=1), transfer))
+def paired(left, right):
+    return jnp.concatenate([left, right], axis=1)
+
+
+def up(pair, transfer):
+    return fold(mt(split(pair), transfer))
 
 
 def packed(x):
@@ -75,17 +79,17 @@
     for handle in handles[:2]:
         handle.wait()
     skel = [mt(halo[g], basis_here[g]) for g in range(8)]
+    pairs = [paired(skel[2 * n], skel[2 * n + 1]) for n in range(4)]
+    for half in range(2):
+        halo[8 + half] = paired(pairs[2 * half], pairs[2 * half + 1]).astype(BF16)
     handles[2].wait()
-    for half in range(2):
-        halo[8 + half] = jnp.concatenate(skel[4 * half : 4 * half + 4], axis=1).astype(BF16)
     offset = 0
-    while len(skel) > 1:
-        parts = [split(x) for x in skel]
-        skel = [
-            up(parts[2 * n], parts[2 * n + 1], local_here[offset + n])
-            for n in range(len(parts) // 2)
-        ]
+    while True:
+        skel = [up(pair, local_here[offset + n]) for n, pair in enumerate(pairs)]
+        if len(skel) == 1:
+            break
         offset += len(skel)
+        pairs = [paired(skel[2 * n], skel[2 * n + 1]) for n in range(len(skel) // 2)]
     root_out[...] = packed(skel[0])
     for handle in handles[3:]:
         handle.wait()
@@ -96,9 +100,8 @@
     own = unpacked(root[...])
     other = unpacked(partner[...])
     sibling[...] = other
-    left = split(jnp.where(odd == 1, other, own))
-    right = split(jnp.where(odd == 1, own, other))
-    merged = packed(up(left, right, transfer[...]))
+    pair = jnp.where(odd == 1, paired(other, own), paired(own, other))
+    merged = packed(up(pair, transfer[...]))
     for peer in range(16):
         message[peer] = merged
 
@@ -121,8 +124,8 @@
 
 def weights_kernel(
     transfer, coupling_in, local_in, basis, blocks, far_coupling,
-    top_out, down_high, down_low, leaf_high, leaf_low, basis_out, blocks_out, far_coupling_out,
-    own_transfer, own_coupling, coupling, local, sems,
+    cross_high, cross_low, down_high, down_low, leaf_high, leaf_low, basis_out, blocks_out,
+    far_coupling_out, top, own_transfer, own_coupling, coupling, local, sems,
 ):
     pos = position()
     copies = [(coupling_in, coupling), (local_in, local)]
@@ -132,7 +135,7 @@
         base += 256 >> level
     early = len(copies)
     copies += [
-        (transfer.at[pl.ds(248, 6)], top_out), (far_coupling, far_coupling_out),
+        (transfer.at[pl.ds(248, 6)], top), (far_coupling, far_coupling_out),
         (basis, basis_out), (blocks, blocks_out),
     ]
     handles = [pltpu.make_async_copy(a, b, sems.at[i]) for i, (a, b) in enumerate(copies)]
@@ -143,8 +146,10 @@
     level_of_row = lax.broadcasted_iota(jnp.int32, (8, 255), 0) + 1
     wanted = 256 - (512 >> level_of_row) + (pos >> level_of_row)
     pick = jnp.where(lax.broadcasted_iota(jnp.int32, (8, 255), 1) == wanted, 1.0, 0.0).astype(BF16)
-    for row in range(64):
-        own_coupling[row] = mt(pick, coupling[row])
+    for row in range(16):
+        found = mt(pick, coupling[4 * row : 4 * row + 4].reshape(256, 255))
+        for part in range(4):
+            own_coupling[4 * row + part] = found[:, 64 * part : 64 * part + 64]
     tops = list(halves_of(local[6].astype(F32)))
     for first, count in ((4, 2), (0, 4)):
         products = []
@@ -157,49 +162,55 @@
     row = lax.broadcasted_iota(jnp.int32, (64, 64), 0)
     col = lax.broadcasted_iota(jnp.int32, (64, 64), 1)
     path = jnp.where(row == col, 1.0, 0.0).astype(F32)
+    terms = []
     for level in range(1, 9):
         side = (pos >> (level - 1)) & 1
         both = split(path)
         block = own_coupling[:, level - 1, :].astype(BF16)
         term = jnp.where(side == 0, fold(mm(both, block)), fold(mt(both, block)))
         down_high[level - 1], down_low[level - 1] = high_low(term)
+        terms.append(term)
         if level < 8:
             left, right = halves_of(own_transfer[level - 1])
             path = fold(mt(both, jnp.where(side == 0, left, right)))
-    for handle in handles[early:]:
+    plane = pos >> 5
+    handles[early].wait()
+    near_node = (plane >> 1) ^ 1
+    far_node = (plane >> 2) ^ 1
+    two = fold(mm(split(terms[6]), top[near_node]))
+    halves = halves_of(fold(mm(split(terms[7]), top[4 + far_node])))
+    fours = [fold(mm(split(half), top[2 * far_node + n])) for n, half in enumerate(halves)]
+    for n, wide in enumerate([two] + fours):
+        cross_high[n], cross_low[n] = high_low(wide)
+    for handle in handles[early + 1 :]:
         handle.wait()
 
 
-def sweep(first, transfer, nodes, levels):
-    parts = first
+def unpacked_pair(left, right):
+    top = jnp.concatenate([left[:, :64], right[:, :64]], axis=1)
+    bottom = jnp.concatenate([left[:, 64:], right[:, 64:]], axis=1)
+    return jnp.concatenate([top, bottom], axis=0)
+
+
+def plane_kernel(received, transfer, message, siblings, nodes):
+    pairs = [unpacked_pair(received[2 * n], received[2 * n + 1]) for n in range(8)]
     offset = 0
-    at = 0
-    for _ in range(levels):
-        count = len(parts) // 2
-        halves = [split(x) for x in parts]
-        parts = [
-            up(halves[2 * n], halves[2 * n + 1], transfer[offset + n]) for n in range(count)
-        ]
-        offset += count
-        at += 2 * count
-        for n in range(count):
-            nodes[at + n] = parts[n]
-    return parts
-
-
-def plane_kernel(received, transfer, message, siblings, nodes):
-    first = [unpacked(received[n]) for n in range(16)]
-    for n in range(16):
-        nodes[n] = first[n]
-    top = sweep(first, transfer, nodes, 4)
-    root = packed(top[0])
+    while True:
+        tops = [up(pair, transfer[offset + n]) for n, pair in enumerate(pairs)]
+        if len(tops) == 1:
+            break
+        for n, top in enumerate(tops):
+            nodes[offset + n] = top
+        offset += len(tops)
+        pairs = [paired(tops[2 * n], tops[2 * n + 1]) for n in range(len(tops) // 2)]
+    root = packed(tops[0])
     for peer in range(8):
         message[peer] = root
     own = (position() >> 1) & 15
-    at = 0
-    for level in range(4):
-        siblings[level] = nodes[at + ((own >> level) ^ 1)]
-        at += 16 >> level
+    siblings[0] = unpacked(received[own ^ 1])
+    siblings[1] = nodes[(own >> 1) ^ 1]
+    siblings[2] = nodes[8 + ((own >> 2) ^ 1)]
+    siblings[3] = nodes[12 + ((own >> 3) ^ 1)]
 
 
 def add_terms(total, siblings, down_high, down_low, first):
@@ -249,19 +260,16 @@
 
 
 def final_kernel(
-    received, transfer, down_high, down_low, leaf_high, leaf_low, coef, near, far, basis, out, nodes,
+    received, cross_high, cross_low, down_high, down_low, leaf_high, leaf_low, coef, near, far, basis,
+    out,
 ):
-    first = [unpacked(received[n]) for n in range(8)]
-    for n in range(8):
-        nodes[n] = first[n]
-    sweep(first, transfer, nodes, 2)
     own = position() >> 5
-    siblings = []
-    at = 0
-    for level in range(3):
-        siblings.append(nodes[at + ((own >> level) ^ 1)])
-        at += 8 >> level
-    total = add_terms(coef[...], siblings, down_high, down_low, 5)
+    two = ((own >> 1) ^ 1) * 2
+    four = ((own >> 2) ^ 1) * 4
+    total = add_terms(coef[...], [unpacked(received[own ^ 1])], down_high, down_low, 5)
+    for n, first in enumerate((two, four, four + 2)):
+        both = split(unpacked_pair(received[first], received[first + 1]))
+        total = total + fold(mt(both, cross_high[n])) + mt(both[:64], cross_low[n])
     both = split(total)
     for pair in range(4):
         coefs = fold(mm(both, leaf_high[pair])) + mm(both[:64], leaf_low[pair])
@@ -319,7 +327,7 @@
     halo, root, first, plane = call(
         leaf_up_kernel, (points, basis, local_transfer, upper_transfer),
         [
-            ((10, 64, 256), BF16, HBM), ((32, 128), F32, VMEM), ((64, 128), BF16, VMEM),
+            ((10, 64, 256), BF16, VMEM), ((32, 128), F32, VMEM), ((64, 128), BF16, VMEM),
             ((15, 64, 128), BF16, VMEM),
         ],
         [HB] * 4,
@@ -334,26 +342,30 @@
     received = exchange(message, (1, 2, 3, 4))
     (pair,) = call(
         assemble_kernel, (halo, partner_halo), [((2, 10, 64, 256), BF16, VMEM)],
-        [HB, ANY], [pltpu.SemaphoreType.DMA((2,))],
+        [ANY, ANY], [pltpu.SemaphoreType.DMA((2,))],
     )
     moved = outward(pair)
     message, siblings = call(
         plane_kernel, (received, plane),
         [((8, 32, 128), F32, HBM), ((4, 64, 64), F32, VMEM)], [VM] * 2,
-        [pltpu.VMEM((31, 64, 64), F32)],
+        [pltpu.VMEM((14, 64, 64), F32)],
     )
     received = exchange(message, (5, 6, 7))
     odd = lax.axis_index("cy") & 1
     passed = swapped(lax.dynamic_slice_in_dim(moved, 1 - odd, 1, 0))
-    top, down_high, down_low, leaf_high, leaf_low, basis, near_blocks, far_coupling = call(
+    (
+        cross_high, cross_low, down_high, down_low, leaf_high, leaf_low, basis, near_blocks,
+        far_coupling,
+    ) = call(
         weights_kernel,
         (upper_transfer, upper_coupling, local_transfer, basis, near_blocks, far_coupling),
-        [((6, 64, 128), BF16, VMEM)] + [((8, 64, 64), BF16, VMEM)] * 2
+        [((3, 64, 128), BF16, VMEM)] * 2 + [((8, 64, 64), BF16, VMEM)] * 2
         + [((4, 64, 128), BF16, VMEM)] * 2
         + [((8, 64, 256), BF16, VMEM), ((8, 4, 256, 256), BF16, VMEM), ((8, 8, 64, 64), BF16, VMEM)],
         [HB] * 6,
         [
-            pltpu.VMEM((8, 64, 128), BF16), pltpu.VMEM((64, 8, 64), F32),
+            pltpu.VMEM((6, 64, 128), BF16), pltpu.VMEM((8, 64, 128), BF16),
+            pltpu.VMEM((64, 8, 64), F32),
             pltpu.VMEM((64, 64, 255), BF16), pltpu.VMEM((7, 64, 128), BF16),
             pltpu.SemaphoreType.DMA((14,)),
         ],
@@ -369,9 +381,8 @@
     )
     (out,) = call(
         final_kernel,
-        (received, top, down_high, down_low, leaf_high, leaf_low, coef, near, far, basis),
-        [((8, 64, 256), BF16, HBM)], [VM] * 10,
-        [pltpu.VMEM((14, 64, 64), F32)],
+        (received, cross_high, cross_low, down_high, down_low, leaf_high, leaf_low, coef, near, far, basis),
+        [((8, 64, 256), BF16, HBM)], [VM] * 11,
     )
     return out
 

time: 48.4 us -> 46.5 us (0.961)
  Pallas kernels: 15.2 us -> 13.9 us
  waiting for transfers between devices: 11 us -> 10.4 us
    pallas_call x7, Pallas kernels: 15.2 us -> 13.9 us  [call(): pl.pallas_call(kernel, out_shape=[space(shape, dtype) for shape, dtype, s...]
  transfers between devices with their start and end apart: 6 -> 6, of which waited for: 5 -> 5; matrix products, arithmetic and copies ran while one was open for 2% -> 2% of each run, Pallas kernels for 19% -> 21%
where the time goes in v1:
time: 46.5 us; the launch traced here: 46.1 us
  starting transfers between devices  20.9 us (45%)
  Pallas kernels  13.9 us (30%)
  waiting for transfers between devices  10.4 us (22%)
  local copies, waits for them, and re-layouts  0.76 us (2%)
    all_to_all x2, starting transfers between devices, exchange(): lax.all_to_all(message, AXES, 0, 0, axis_index_groups=groups_of(bits))  15.4 us
    pallas_call x7, Pallas kernels, call(): pl.pallas_call(kernel, out_shape=[space(shape, dtype) for shape, dtype, s...  13.9 us
    all_to_all x2, waiting for transfers between devices, exchange(): lax.all_to_all(message, AXES, 0, 0, axis_index_groups=groups_of(bits))  7.51 us
    ppermute x3, starting transfers between devices, swapped(): lax.ppermute(value, AXES, [(i, i ^ 1) for i in range(lax.axis_size(AXES))])  4.19 us
    ppermute x3, waiting for transfers between devices, swapped(): lax.ppermute(value, AXES, [(i, i ^ 1) for i in range(lax.axis_size(AXES))])  2.1 us
    ppermute x1, starting transfers between devices, outward(): lax.ppermute(value, AXES, [(i, j) for i, j in pairs if 0 <= j < count])  1.29 us
  transfers between devices with their start and end apart: 6, of which 5 were waited for; matrix products, arithmetic and copies ran while one was open for 2% of the time, Pallas kernels for 21%

profile of v1, /device:TPU:1, one launch (start us, length us, event | category | flops | bytes accessed | tf_op | source)
XLA Modules:
  0.0 46.1 jit_solution(10100757809957794762)
XLA Ops:
  0.0 2.0 %shard_map.91 = (bf16[10,64,256]{2,1,0:T(8,128)(2,1)S(1)}, f32[32,128]{1,0:T(8,128)S(1)}, bf16[64,128]{1,0:T(8,128)(2,1)S(1)}, bf16[15,64,128]{2,1,0:T(8,128)(2,1)S(1)}) custom-call(bf16[8,64,256]{2,1,0:T(8,128)(2,1)} %points.1, bf16[8,64,256]{2,1,0:T(8,128)(2,1)} %basis.3, bf16[7,64,128]{2,1,0:T(8,128)(2,1)} %bitcast.8, bf16[255,64,128]{2,1,0:T(8,128)(2,1)} %bitcast.5), custom_call_target="tpu_custom_call" | custom-call | tf_op jit(solution)/shard_map/pallas_call | solution.py:287
  2.0 3.3 %collective-permute-start.1 = (bf16[10,64,256]{2,1,0:T(8,128)(2,1)S(1)}, bf16[10,64,256]{2,1,0:T(8,128)(2,1)S(1)}, u32[]{:S(2)}, u32[]{:S(2)}) collective-permute-start(bf16[10,64,256]{2,1,0:T(8,128)(2,1)S(1)} %get-tuple-element.36.halo), channel_id=1, source_target_pairs={{0,1},{1,0},{2,3},{3,2},{4,5},{5,4},{6,7},{7,6},{8,9},{9,8},{10,11... | collective-permute-start | bytes 983048 | tf_op jit(solution)/shard_map/ppermute | solution.py:310
  5.3 1.3 %collective-permute-done.1.partner = bf16[10,64,256]{2,1,0:T(8,128)(2,1)S(1)} collective-permute-done((bf16[10,64,256]{2,1,0:T(8,128)(2,1)S(1)}, bf16[10,64,256]{2,1,0:T(8,128)(2,1)S(1)}, u32[]{:S(2)}, u32[]{:S(2)}) %collective-permute-start.1) | collective-permute-done | bytes 327712 | tf_op jit(solution)/shard_map/ppermute | solution.py:310
  6.6 0.2 shard_map.95.pair
  6.8 1.3 %collective-permute-start.2 = (bf16[2,10,64,256]{3,2,1,0:T(8,128)(2,1)S(1)}, bf16[2,10,64,256]{3,2,1,0:T(8,128)(2,1)S(1)}, u32[]{:S(2)}, u32[]{:S(2)}) collective-permute-start(bf16[2,10,64,256]{3,2,1,0:T(8,128)(2,1)S(1)} %shard_map.95.pair), channel_id=1, source_target_pairs={{0,2},{2,4},{3,1},{4,6},{5,3},{6,8},{7,5},{8,10},{9,7},{10,12},{11... | collective-permute-start | bytes 1966088 | tf_op jit(solution)/shard_map/ppermute | solution.py:316
  8.1 0.9 %collective-permute-start = (f32[32,128]{1,0:T(8,128)S(1)}, f32[32,128]{1,0:T(8,128)S(1)}, u32[]{:S(2)}, u32[]{:S(2)}) collective-permute-start(f32[32,128]{1,0:T(8,128)S(1)} %get-tuple-element.25.root), channel_id=1, source_target_pairs={{0,1},{1,0},{2,3},{3,2},{4,5},{5,4},{6,7},{7,6},{8,9},{9,8},{10,11... | collective-permute-start | bytes 49160 | tf_op jit(solution)/shard_map/ppermute | solution.py:310
  9.0 0.8 %collective-permute-done.partner = f32[32,128]{1,0:T(8,128)S(1)} collective-permute-done((f32[32,128]{1,0:T(8,128)S(1)}, f32[32,128]{1,0:T(8,128)S(1)}, u32[]{:S(2)}, u32[]{:S(2)}) %collective-permute-start) | collective-permute-done | bytes 16416 | tf_op jit(solution)/shard_map/ppermute | solution.py:310
  9.8 1.1 %shard_map.92 = (f32[16,32,128]{2,1,0:T(8,128)}, f32[64,64]{1,0:T(8,128)S(1)}) custom-call(f32[32,128]{1,0:T(8,128)S(1)} %get-tuple-element.25.root, f32[32,128]{1,0:T(8,128)S(1)} %collective-permute-done.partner, bf16[64,128]{1,0:T(8,128)(2,1)S(1)} %get-tuple-element.26.transfer), custom_call_target="tpu_custom_call" | custom-call | tf_op jit(solution)/shard_map/pallas_call | solution.py:287
  10.9 6.4 %all-to-all-start = ((f32[16,32,128]{2,1,0:T(8,128)}), f32[16,32,128]{2,1,0:T(8,128)S(1)}, u32[]{:S(2)}, u32[]{:S(2)}) async-start(f32[16,32,128]{2,1,0:T(8,128)} %get-tuple-element.27), calls=%async_computation | async-start | bytes 524288 | tf_op jit(solution)/shard_map/all_to_all | solution.py:306
  17.3 0.8 %collective-permute-done.2.moved = bf16[2,10,64,256]{3,2,1,0:T(8,128)(2,1)S(1)} collective-permute-done((bf16[2,10,64,256]{3,2,1,0:T(8,128)(2,1)S(1)}, bf16[2,10,64,256]{3,2,1,0:T(8,128)(2,1)S(1)}, u32[]{:S(2)}, u32[]{:S(2)}) %collective-permute-start.2) | collective-permute-done | bytes 655392 | tf_op jit(solution)/shard_map/ppermute | solution.py:316
  18.1 0.7 %constant_dynamic-slice_fusion = bf16[1,10,64,256]{3,2,1,0:T(8,128)(2,1)} fusion(bf16[2,10,64,256]{3,2,1,0:T(8,128)(2,1)S(1)} %collective-permute-done.2.moved, s32[]{:T(128)S(6)} %select_n.3), kind=kLoop, calls=%fused_computation | loop fusion | bytes 655364 | tf_op jit(solution)/shard_map/dynamic_slice | solution.py:355
  18.9 0.0 collective-permute-start.3
  18.9 6.6 %all-to-all-done.received = f32[16,32,128]{2,1,0:T(8,128)S(1)} async-done(((f32[16,32,128]{2,1,0:T(8,128)}), f32[16,32,128]{2,1,0:T(8,128)S(1)}, u32[]{:S(2)}, u32[]{:S(2)}) %all-to-all-start) | async-done | bytes 262176 | tf_op jit(solution)/shard_map/all_to_all | solution.py:306
  25.5 1.6 %shard_map.93 = (f32[8,32,128]{2,1,0:T(8,128)}, f32[4,64,64]{2,1,0:T(8,128)S(1)}) custom-call(f32[16,32,128]{2,1,0:T(8,128)S(1)} %all-to-all-done.received, bf16[15,64,128]{2,1,0:T(8,128)(2,1)S(1)} %get-tuple-element.28.transfer), custom_call_target="tpu_custom_call" | custom-call | tf_op jit(solution)/shard_map/pallas_call | solution.py:287
  27.1 9.0 %all-to-all-start.1 = ((f32[8,32,128]{2,1,0:T(8,128)}), f32[8,32,128]{2,1,0:T(8,128)S(1)}, u32[]{:S(2)}, u32[]{:S(2)}) async-start(f32[8,32,128]{2,1,0:T(8,128)} %get-tuple-element.29), calls=%async_computation.1 | async-start | bytes 262144 | tf_op jit(solution)/shard_map/all_to_all | solution.py:306
  36.1 0.0 copy-start
  36.1 0.0 copy-start.1
  36.1 4.5 %shard_map.94 = (bf16[3,64,128]{2,1,0:T(8,128)(2,1)S(1)}, bf16[3,64,128]{2,1,0:T(8,128)(2,1)S(1)}, bf16[8,64,64]{2,1,0:T(8,128)(2,1)S(1)}, bf16[8,64,64]{2,1,0:T...) custom-call(bf16[255,64,128]{2,1,0:T(8,128)(2,1)} %bitcast.6, ...), custom_call_target="tpu_custom_call" | custom-call | tf_op jit(solution)/shard_map/pallas_call | solution.py:287
  40.6 0.0 collective-permute-done.3.passed
  40.6 0.0 copy-done
  40.6 0.0 copy-done.1
  40.6 2.6 %shard_map.96 = (f32[8,64,256]{2,1,0:T(8,128)S(1)}, f32[8,64,64]{2,1,0:T(8,128)S(1)}, f32[64,64]{1,0:T(8,128)S(1)}) custom-call(s32[4,8]{1,0:T(4,128)S(1)} %bitcast.4, s32[8,8]{1,0:T(8,128)S(1)} %copy-done, bf16[2,10,64,256]{3,2,1,0:T(8,128)(2,1)S(1)} %shard_map.95.pair, bf16[2,10,64,256]{3,2,1,0:T(8,128)(2,1)S(1)} %collective-permute-done.2.moved, ...), custom_call_target="tpu_custom_call" | custom-call | tf_op jit(solution)/shard_map/pallas_call | solution.py:287
  43.2 0.9 %all-to-all-done.1.received = f32[8,32,128]{2,1,0:T(8,128)S(1)} async-done(((f32[8,32,128]{2,1,0:T(8,128)}), f32[8,32,128]{2,1,0:T(8,128)S(1)}, u32[]{:S(2)}, u32[]{:S(2)}) %all-to-all-start.1) | async-done | bytes 131104 | tf_op jit(solution)/shard_map/all_to_all | solution.py:306
  44.1 2.0 %shard_map.97 = bf16[8,64,256]{2,1,0:T(8,128)(2,1)} custom-call(f32[8,32,128]{2,1,0:T(8,128)S(1)} %all-to-all-done.1.received, bf16[3,64,128]{2,1,0:T(8,128)(2,1)S(1)} %get-tuple-element.30.cross_high, bf16[3,64,128]{2,1,0:T(8,128)(2,1)S(1)} %get-tuple-element.31.cross_low, bf16[8,64,64]{2,1,0:T(8,128)(2,1)S(1)} %get-tuple-element.32.down_high, ...), custom_call_target="tpu_custom_call" | custom-call | tf_op jit(solution)/shard_map/pallas_call | solution.py:287
Async XLA Ops:
  2.0 4.5 %collective-permute-start.1 = (bf16[10,64,256]{2,1,0:T(8,128)(2,1)S(1)}, bf16[10,64,256]{2,1,0:T(8,128)(2,1)S(1)}, u32[]{:S(2)}, u32[]{:S(2)}) collective-permute-start(bf16[10,64,256]{2,1,0:T(8,128)(2,1)S(1)} %get-tuple-element.36.halo), channel_id=1, source_target_pairs={{0,1},{1,0},{2,3},{3,2},{4,5},{5,4},{6,7},{7,6},{8,9},{9,8},{10,11... | collective-permute-start | bytes 983048 | tf_op jit(solution)/shard_map/ppermute | solution.py:310
  6.8 11.3 %collective-permute-start.2 = (bf16[2,10,64,256]{3,2,1,0:T(8,128)(2,1)S(1)}, bf16[2,10,64,256]{3,2,1,0:T(8,128)(2,1)S(1)}, u32[]{:S(2)}, u32[]{:S(2)}) collective-permute-start(bf16[2,10,64,256]{3,2,1,0:T(8,128)(2,1)S(1)} %shard_map.95.pair), channel_id=1, source_target_pairs={{0,2},{2,4},{3,1},{4,6},{5,3},{6,8},{7,5},{8,10},{9,7},{10,12},{11... | collective-permute-start | bytes 1966088 | tf_op jit(solution)/shard_map/ppermute | solution.py:316
  8.1 1.7 %collective-permute-start = (f32[32,128]{1,0:T(8,128)S(1)}, f32[32,128]{1,0:T(8,128)S(1)}, u32[]{:S(2)}, u32[]{:S(2)}) collective-permute-start(f32[32,128]{1,0:T(8,128)S(1)} %get-tuple-element.25.root), channel_id=1, source_target_pairs={{0,1},{1,0},{2,3},{3,2},{4,5},{5,4},{6,7},{7,6},{8,9},{9,8},{10,11... | collective-permute-start | bytes 49160 | tf_op jit(solution)/shard_map/ppermute | solution.py:310
  10.9 14.6 %all-to-all-start = ((f32[16,32,128]{2,1,0:T(8,128)}), f32[16,32,128]{2,1,0:T(8,128)S(1)}, u32[]{:S(2)}, u32[]{:S(2)}) async-start(f32[16,32,128]{2,1,0:T(8,128)} %get-tuple-element.27), calls=%async_computation | async-start | bytes 524288 | tf_op jit(solution)/shard_map/all_to_all | solution.py:306
  18.9 21.7 %collective-permute-start.3 = (bf16[1,10,64,256]{3,2,1,0:T(8,128)(2,1)}, bf16[1,10,64,256]{3,2,1,0:T(8,128)(2,1)S(1)}, u32[]{:S(2)}, u32[]{:S(2)}) collective-permute-start(bf16[1,10,64,256]{3,2,1,0:T(8,128)(2,1)} %constant_dynamic-slice_fusion), channel_id=1, source_target_pairs={{0,1},{1,0},{2,3},{3,2},{4,5},{5,4},{6,7},{7,6},{8,9},{9,8},{10,11... | collective-permute-start | bytes 983048 | tf_op jit(solution)/shard_map/ppermute | solution.py:310
  27.1 17.0 %all-to-all-start.1 = ((f32[8,32,128]{2,1,0:T(8,128)}), f32[8,32,128]{2,1,0:T(8,128)S(1)}, u32[]{:S(2)}, u32[]{:S(2)}) async-start(f32[8,32,128]{2,1,0:T(8,128)} %get-tuple-element.29), calls=%async_computation.1 | async-start | bytes 262144 | tf_op jit(solution)/shard_map/all_to_all | solution.py:306
  36.1 4.5 %copy-start = (s32[8,8]{1,0:T(8,128)S(1)}, s32[8,8]{1,0:T(8,128)}, u32[]{:S(2)}) copy-start(s32[8,8]{1,0:T(8,128)} %far_ids.1) | copy-start | bytes 772
  36.1 4.5 %copy-start.1 = (s32[8,4]{0,1:T(4,128)S(1)}, s32[8,4]{0,1:T(4,128)}, u32[]{:S(2)}) copy-start(s32[8,4]{0,1:T(4,128)} %param.12) | copy-start | bytes 388

commit v2 on v1

--- a/solution.py
+++ b/solution.py
@@ -42,12 +42,29 @@
     return y[:half] + y[half:]
 
 
+def halves_of(x):
+    return x[:, :64], x[:, 64:]
+
+
 def paired(left, right):
     return jnp.concatenate([left, right], axis=1)
 
 
-def up(pair, transfer):
-    return fold(mt(split(pair), transfer))
+def up(left, right, transfer):
+    return fold(mt(split(left), transfer[0]) + mt(split(right), transfer[1]))
+
+
+def up_packed(left, right, wide):
+    return fold(mt(split(paired(left, right)), wide))
+
+
+def widened(transfer):
+    low = (lax.broadcasted_iota(jnp.int32, (64, 128), 1) < 64).astype(F32).astype(BF16)
+    high = (lax.broadcasted_iota(jnp.int32, (64, 128), 1) >= 64).astype(F32).astype(BF16)
+    turned = jnp.concatenate([transfer[:, 64:], transfer[:, :64]], axis=1)
+    top = paired(transfer * low, turned * low)
+    bottom = paired(turned * high, transfer * high)
+    return jnp.concatenate([top, bottom], axis=0)
 
 
 def packed(x):
@@ -59,13 +76,14 @@
 
 
 def leaf_up_kernel(
-    points, basis, local, transfer, halo, root_out, first_out, plane_out, basis_here, local_here, sems
+    points, basis, local, transfer, halo, root_out, first_out, plane_out, basis_here, local_here,
+    first_here, sems,
 ):
     pos = position()
     plane = pos >> 5
     copies = [
         (points, halo.at[pl.ds(0, 8)]), (basis, basis_here), (local, local_here),
-        (transfer.at[pos >> 1], first_out),
+        (transfer.at[pos >> 1], first_here),
     ]
     base = 128
     at = 0
@@ -79,29 +97,31 @@
     for handle in handles[:2]:
         handle.wait()
     skel = [mt(halo[g], basis_here[g]) for g in range(8)]
-    pairs = [paired(skel[2 * n], skel[2 * n + 1]) for n in range(4)]
     for half in range(2):
-        halo[8 + half] = paired(pairs[2 * half], pairs[2 * half + 1]).astype(BF16)
+        halo[8 + half] = jnp.concatenate(skel[4 * half : 4 * half + 4], axis=1).astype(BF16)
     handles[2].wait()
     offset = 0
-    while True:
-        skel = [up(pair, local_here[offset + n]) for n, pair in enumerate(pairs)]
-        if len(skel) == 1:
-            break
+    while len(skel) > 1:
+        skel = [
+            up(skel[2 * n], skel[2 * n + 1], halves_of(local_here[offset + n]))
+            for n in range(len(skel) // 2)
+        ]
         offset += len(skel)
-        pairs = [paired(skel[2 * n], skel[2 * n + 1]) for n in range(len(skel) // 2)]
-    root_out[...] = packed(skel[0])
-    for handle in handles[3:]:
+    root_out[...] = skel[0]
+    handles[3].wait()
+    first_out[0], first_out[1] = halves_of(first_here[...])
+    for handle in handles[4:]:
         handle.wait()
 
 
 def merge_kernel(root, partner, transfer, message, sibling):
     odd = position() & 1
-    own = unpacked(root[...])
-    other = unpacked(partner[...])
+    own = root[...]
+    other = partner[...]
     sibling[...] = other
-    pair = jnp.where(odd == 1, paired(other, own), paired(own, other))
-    merged = packed(up(pair, transfer[...]))
+    left = jnp.where(odd == 1, other, own)
+    right = jnp.where(odd == 1, own, other)
+    merged = packed(up(left, right, (transfer[0], transfer[1]))).astype(BF16)
     for peer in range(16):
         message[peer] = merged
 
@@ -118,14 +138,10 @@
         handle.wait()
 
 
-def halves_of(x):
-    return x[:, :64], x[:, 64:]
-
-
 def weights_kernel(
     transfer, coupling_in, local_in, basis, blocks, far_coupling,
-    cross_high, cross_low, down_high, down_low, leaf_high, leaf_low, basis_out, blocks_out,
-    far_coupling_out, top, own_transfer, own_coupling, coupling, local, sems,
+    next_high, next_low, cross_high, cross_low, down_high, down_low, leaf_high, leaf_low, basis_out,
+    blocks_out, far_coupling_out, top, own_transfer, own_coupling, coupling, local, sems,
 ):
     pos = position()
     copies = [(coupling_in, coupling), (local_in, local)]
@@ -181,33 +197,38 @@
     halves = halves_of(fold(mm(split(terms[7]), top[4 + far_node])))
     fours = [fold(mm(split(half), top[2 * far_node + n])) for n, half in enumerate(halves)]
     for n, wide in enumerate([two] + fours):
-        cross_high[n], cross_low[n] = high_low(wide)
+        high, low = high_low(wide)
+        cross_high[n], cross_low[n] = widened(high), widened(low)
+    zero = jnp.zeros((64, 64), BF16)
+    for out, part in zip((next_high, next_low), high_low(terms[5])):
+        out[:64] = paired(part, zero)
+        out[64:] = paired(zero, part)
     for handle in handles[early + 1 :]:
         handle.wait()
 
 
-def unpacked_pair(left, right):
-    top = jnp.concatenate([left[:, :64], right[:, :64]], axis=1)
-    bottom = jnp.concatenate([left[:, 64:], right[:, 64:]], axis=1)
-    return jnp.concatenate([top, bottom], axis=0)
-
-
-def plane_kernel(received, transfer, message, siblings, nodes):
-    pairs = [unpacked_pair(received[2 * n], received[2 * n + 1]) for n in range(8)]
+def widen_kernel(transfer, wide):
+    for n in range(15):
+        wide[n] = widened(transfer[n])
+
+
+def plane_kernel(received, wide, message, siblings, nodes):
+    tops = [mt(paired(received[2 * n], received[2 * n + 1]), wide[n]) for n in range(8)]
     offset = 0
     while True:
-        tops = [up(pair, transfer[offset + n]) for n, pair in enumerate(pairs)]
         if len(tops) == 1:
             break
         for n, top in enumerate(tops):
             nodes[offset + n] = top
         offset += len(tops)
-        pairs = [paired(tops[2 * n], tops[2 * n + 1]) for n in range(len(tops) // 2)]
-    root = packed(tops[0])
+        tops = [
+            up_packed(tops[2 * n], tops[2 * n + 1], wide[offset + n]) for n in range(len(tops) // 2)
+        ]
+    root = tops[0].astype(BF16)
     for peer in range(8):
         message[peer] = root
     own = (position() >> 1) & 15
-    siblings[0] = unpacked(received[own ^ 1])
+    siblings[0] = received[own ^ 1].astype(F32)
     siblings[1] = nodes[(own >> 1) ^ 1]
     siblings[2] = nodes[8 + ((own >> 2) ^ 1)]
     siblings[3] = nodes[12 + ((own >> 3) ^ 1)]
@@ -227,10 +248,10 @@
     pos = position()
     odd = pos & 1
     pair_at, moved_at, passed_at = 2 - odd, 3 * odd, 4 - 4 * odd
-    coef_out[...] = add_terms(
-        jnp.zeros((64, 64), F32), [sibling[...]] + [siblings[n] for n in range(4)],
+    coef_out[...] = packed(add_terms(
+        jnp.zeros((64, 64), F32), [sibling[...]] + [unpacked(siblings[n]) for n in range(4)],
         down_high, down_low, 0,
-    )
+    ))
     first_leaf = (pos - 2) * 8
     for source, at, count in ((pair, pair_at, 2), (moved, moved_at, 2), (passed, passed_at, 1)):
         for device in range(count):
@@ -260,16 +281,18 @@
 
 
 def final_kernel(
-    received, cross_high, cross_low, down_high, down_low, leaf_high, leaf_low, coef, near, far, basis,
+    received, next_high, next_low, cross_high, cross_low, leaf_high, leaf_low, coef, near, far, basis,
     out,
 ):
     own = position() >> 5
     two = ((own >> 1) ^ 1) * 2
     four = ((own >> 2) ^ 1) * 4
-    total = add_terms(coef[...], [unpacked(received[own ^ 1])], down_high, down_low, 5)
+    one = received[own ^ 1]
+    total = coef[...] + mt(one, next_high[...]) + mt(one, next_low[...])
     for n, first in enumerate((two, four, four + 2)):
-        both = split(unpacked_pair(received[first], received[first + 1]))
-        total = total + fold(mt(both, cross_high[n])) + mt(both[:64], cross_low[n])
+        pair = paired(received[first], received[first + 1])
+        total = total + mt(pair, cross_high[n]) + mt(pair, cross_low[n])
+    total = unpacked(total)
     both = split(total)
     for pair in range(4):
         coefs = fold(mm(both, leaf_high[pair])) + mm(both[:64], leaf_low[pair])
@@ -327,17 +350,20 @@
     halo, root, first, plane = call(
         leaf_up_kernel, (points, basis, local_transfer, upper_transfer),
         [
-            ((10, 64, 256), BF16, VMEM), ((32, 128), F32, VMEM), ((64, 128), BF16, VMEM),
+            ((10, 64, 256), BF16, VMEM), ((64, 64), F32, VMEM), ((2, 64, 64), BF16, VMEM),
             ((15, 64, 128), BF16, VMEM),
         ],
         [HB] * 4,
-        [pltpu.VMEM((8, 64, 256), BF16), pltpu.VMEM((7, 64, 128), BF16), pltpu.SemaphoreType.DMA((8,))],
+        [
+            pltpu.VMEM((8, 64, 256), BF16), pltpu.VMEM((7, 64, 128), BF16),
+            pltpu.VMEM((64, 128), BF16), pltpu.SemaphoreType.DMA((8,)),
+        ],
     )
     partner = swapped(root)
     partner_halo = swapped(halo)
     message, sibling = call(
         merge_kernel, (root, partner, first),
-        [((16, 32, 128), F32, HBM), ((64, 64), F32, VMEM)], [VM] * 3,
+        [((16, 32, 128), BF16, HBM), ((64, 64), F32, VMEM)], [VM] * 3,
     )
     received = exchange(message, (1, 2, 3, 4))
     (pair,) = call(
@@ -345,21 +371,23 @@
         [ANY, ANY], [pltpu.SemaphoreType.DMA((2,))],
     )
     moved = outward(pair)
+    (wide,) = call(widen_kernel, (plane,), [((15, 128, 256), BF16, VMEM)], [VM])
     message, siblings = call(
-        plane_kernel, (received, plane),
-        [((8, 32, 128), F32, HBM), ((4, 64, 64), F32, VMEM)], [VM] * 2,
-        [pltpu.VMEM((14, 64, 64), F32)],
+        plane_kernel, (received, wide),
+        [((8, 32, 128), BF16, HBM), ((4, 32, 128), F32, VMEM)], [VM] * 2,
+        [pltpu.VMEM((14, 32, 128), F32)],
     )
     received = exchange(message, (5, 6, 7))
     odd = lax.axis_index("cy") & 1
     passed = swapped(lax.dynamic_slice_in_dim(moved, 1 - odd, 1, 0))
     (
-        cross_high, cross_low, down_high, down_low, leaf_high, leaf_low, basis, near_blocks,
-        far_coupling,
+        next_high, next_low, cross_high, cross_low, down_high, down_low, leaf_high, leaf_low,
+        basis, near_blocks, far_coupling,
     ) = call(
         weights_kernel,
         (upper_transfer, upper_coupling, local_transfer, basis, near_blocks, far_coupling),
-        [((3, 64, 128), BF16, VMEM)] * 2 + [((8, 64, 64), BF16, VMEM)] * 2
+        [((128, 128), BF16, VMEM)] * 2 + [((3, 128, 256), BF16, VMEM)] * 2
+        + [((8, 64, 64), BF16, VMEM)] * 2
         + [((4, 64, 128), BF16, VMEM)] * 2
         + [((8, 64, 256), BF16, VMEM), ((8, 4, 256, 256), BF16, VMEM), ((8, 8, 64, 64), BF16, VMEM)],
         [HB] * 6,
@@ -375,13 +403,14 @@
         near_far_kernel,
         (near_ids, far_ids, pair, moved, passed, near_blocks, far_coupling, sibling, siblings,
          down_high, down_low),
-        [((8, 64, 256), F32, VMEM), ((8, 64, 64), F32, VMEM), ((64, 64), F32, VMEM)],
+        [((8, 64, 256), F32, VMEM), ((8, 64, 64), F32, VMEM), ((32, 128), F32, VMEM)],
         [SM, SM] + [VM] * 9,
         [pltpu.VMEM((40, 64, 64), BF16)],
     )
     (out,) = call(
         final_kernel,
-        (received, cross_high, cross_low, down_high, down_low, leaf_high, leaf_low, coef, near, far, basis),
+        (received, next_high, next_low, cross_high, cross_low, leaf_high, leaf_low, coef, near, far,
+         basis),
         [((8, 64, 256), BF16, HBM)], [VM] * 11,
     )
     return out

time: 46.5 us -> 57 us (1.23)
  waiting for transfers between devices: 10.4 us -> 19.4 us
  starting transfers between devices: 20.9 us -> 22.1 us
    ppermute x1, waiting for transfers between devices: 0.8 us -> 10 us  [outward(): lax.ppermute(value, AXES, [(i, j) for i, j in pairs if 0 <= j < count])]
    all_to_all x2, starting transfers between devices: 15.4 us -> 17 us  [exchange(): lax.all_to_all(message, AXES, 0, 0, axis_index_groups=groups_of(bits))]
    all_to_all x2, waiting for transfers between devices: 7.51 us -> 6.79 us  [exchange(): lax.all_to_all(message, AXES, 0, 0, axis_index_groups=groups_of(bits))]
    pallas_call x7 -> x8, Pallas kernels: 13.9 us -> 13.8 us  [call(): pl.pallas_call(kernel, out_shape=[space(shape, dtype) for shape, dtype, s...]
  transfers between devices with their start and end apart: 6 -> 6, of which waited for: 5 -> 5; matrix products, arithmetic and copies ran while one was open for 2% -> 0% of each run, Pallas kernels for 21% -> 17%
where the time goes in v2:
time: 57 us; the launch traced here: 56.2 us
  starting transfers between devices  22.1 us (39%)
  waiting for transfers between devices  19.4 us (34%)
  Pallas kernels  13.8 us (24%)
  local copies, waits for them, and re-layouts  0.76 us (1%)
    all_to_all x2, starting transfers between devices, exchange(): lax.all_to_all(message, AXES, 0, 0, axis_index_groups=groups_of(bits))  17 us
    pallas_call x8, Pallas kernels, call(): pl.pallas_call(kernel, out_shape=[space(shape, dtype) for shape, dtype, s...  13.8 us
    ppermute x1, waiting for transfers between devices, outward(): lax.ppermute(value, AXES, [(i, j) for i, j in pairs if 0 <= j < count])  10 us
    all_to_all x2, waiting for transfers between devices, exchange(): lax.all_to_all(message, AXES, 0, 0, axis_index_groups=groups_of(bits))  6.79 us
    ppermute x3, starting transfers between devices, swapped(): lax.ppermute(value, AXES, [(i, i ^ 1) for i in range(lax.axis_size(AXES))])  3.8 us
    ppermute x3, waiting for transfers between devices, swapped(): lax.ppermute(value, AXES, [(i, i ^ 1) for i in range(lax.axis_size(AXES))])  2.63 us
    ppermute x1, starting transfers between devices, outward(): lax.ppermute(value, AXES, [(i, j) for i, j in pairs if 0 <= j < count])  1.29 us
  transfers between devices with their start and end apart: 6, of which 5 were waited for; matrix products, arithmetic and copies ran while one was open for 0% of the time, Pallas kernels for 17%

profile of v2, /device:TPU:1, one launch (start us, length us, event | category | flops | bytes accessed | tf_op | source)
XLA Modules:
  0.0 56.2 jit_solution(3709498207930422944)
XLA Ops:
  0.0 2.1 %shard_map.91 = (bf16[10,64,256]{2,1,0:T(8,128)(2,1)S(1)}, f32[64,64]{1,0:T(8,128)S(1)}, bf16[2,64,64]{2,1,0:T(8,128)(2,1)S(1)}, bf16[15,64,128]{2,1,0:T(8,128)(2,1)S(1)}) custom-call(bf16[8,64,256]{2,1,0:T(8,128)(2,1)} %points.1, bf16[8,64,256]{2,1,0:T(8,128)(2,1)} %basis.3, bf16[7,64,128]{2,1,0:T(8,128)(2,1)} %bitcast.8, bf16[255,64,128]{2,1,0:T(8,128)(2,1)} %bitcast.5), custom_call_target="tpu_custom_call" | custom-call | tf_op jit(solution)/shard_map/pallas_call | solution.py:310
  2.1 3.3 %collective-permute-start.1 = (bf16[10,64,256]{2,1,0:T(8,128)(2,1)S(1)}, bf16[10,64,256]{2,1,0:T(8,128)(2,1)S(1)}, u32[]{:S(2)}, u32[]{:S(2)}) collective-permute-start(bf16[10,64,256]{2,1,0:T(8,128)(2,1)S(1)} %get-tuple-element.38.halo), channel_id=1, source_target_pairs={{0,1},{1,0},{2,3},{3,2},{4,5},{5,4},{6,7},{7,6},{8,9},{9,8},{10,11... | collective-permute-start | bytes 983048 | tf_op jit(solution)/shard_map/ppermute | solution.py:333
  5.4 1.3 %collective-permute-done.1.partner = bf16[10,64,256]{2,1,0:T(8,128)(2,1)S(1)} collective-permute-done((bf16[10,64,256]{2,1,0:T(8,128)(2,1)S(1)}, bf16[10,64,256]{2,1,0:T(8,128)(2,1)S(1)}, u32[]{:S(2)}, u32[]{:S(2)}) %collective-permute-start.1) | collective-permute-done | bytes 327712 | tf_op jit(solution)/shard_map/ppermute | solution.py:333
  6.6 0.2 shard_map.96.pair
  6.8 1.3 %collective-permute-start.2 = (bf16[2,10,64,256]{3,2,1,0:T(8,128)(2,1)S(1)}, bf16[2,10,64,256]{3,2,1,0:T(8,128)(2,1)S(1)}, u32[]{:S(2)}, u32[]{:S(2)}) collective-permute-start(bf16[2,10,64,256]{3,2,1,0:T(8,128)(2,1)S(1)} %shard_map.96.pair), channel_id=1, source_target_pairs={{0,2},{2,4},{3,1},{4,6},{5,3},{6,8},{7,5},{8,10},{9,7},{10,12},{11... | collective-permute-start | bytes 1966088 | tf_op jit(solution)/shard_map/ppermute | solution.py:339
  8.1 10.0 %collective-permute-done.2.moved = bf16[2,10,64,256]{3,2,1,0:T(8,128)(2,1)S(1)} collective-permute-done((bf16[2,10,64,256]{3,2,1,0:T(8,128)(2,1)S(1)}, bf16[2,10,64,256]{3,2,1,0:T(8,128)(2,1)S(1)}, u32[]{:S(2)}, u32[]{:S(2)}) %collective-permute-start.2) | collective-permute-done | bytes 655392 | tf_op jit(solution)/shard_map/ppermute | solution.py:339
  18.2 0.7 %constant_dynamic-slice_fusion = bf16[1,10,64,256]{3,2,1,0:T(8,128)(2,1)} fusion(bf16[2,10,64,256]{3,2,1,0:T(8,128)(2,1)S(1)} %collective-permute-done.2.moved, s32[]{:T(128)S(6)} %select_n.3), kind=kLoop, calls=%fused_computation | loop fusion | bytes 655364 | tf_op jit(solution)/shard_map/dynamic_slice | solution.py:382
  18.9 0.0 collective-permute-start.3
  18.9 0.5 collective-permute-start
  19.4 1.4 %collective-permute-done.partner = f32[64,64]{1,0:T(8,128)S(1)} collective-permute-done((f32[64,64]{1,0:T(8,128)S(1)}, f32[64,64]{1,0:T(8,128)S(1)}, u32[]{:S(2)}, u32[]{:S(2)}) %collective-permute-start) | collective-permute-done | bytes 16416 | tf_op jit(solution)/shard_map/ppermute | solution.py:333
  20.8 0.9 %shard_map.92 = (bf16[16,32,128]{2,1,0:T(8,128)(2,1)}, f32[64,64]{1,0:T(8,128)S(1)}) custom-call(f32[64,64]{1,0:T(8,128)S(1)} %get-tuple-element.27.root, f32[64,64]{1,0:T(8,128)S(1)} %collective-permute-done.partner, bf16[2,64,64]{2,1,0:T(8,128)(2,1)S(1)} %get-tuple-element.28.transfer), custom_call_target="tpu_custom_call" | custom-call | tf_op jit(solution)/shard_map/pallas_call | solution.py:310
  21.7 8.8 %all-to-all-start = ((bf16[16,32,128]{2,1,0:T(8,128)(2,1)}), bf16[16,32,128]{2,1,0:T(8,128)(2,1)S(1)}, u32[]{:S(2)}, u32[]{:S(2)}) async-start(bf16[16,32,128]{2,1,0:T(8,128)(2,1)} %get-tuple-element.29), calls=%async_computation | async-start | bytes 262144 | tf_op jit(solution)/shard_map/all_to_all | solution.py:329
  30.5 0.2 shard_map.93.wide
  30.7 6.7 %all-to-all-done.received = bf16[16,32,128]{2,1,0:T(8,128)(2,1)S(1)} async-done(((bf16[16,32,128]{2,1,0:T(8,128)(2,1)}), bf16[16,32,128]{2,1,0:T(8,128)(2,1)S(1)}, u32[]{:S(2)}, u32[]{:S(2)}) %all-to-all-start) | async-done | bytes 131104 | tf_op jit(solution)/shard_map/all_to_all | solution.py:329
  37.4 1.3 %shard_map.94 = (bf16[8,32,128]{2,1,0:T(8,128)(2,1)}, f32[4,32,128]{2,1,0:T(8,128)S(1)}) custom-call(bf16[16,32,128]{2,1,0:T(8,128)(2,1)S(1)} %all-to-all-done.received, bf16[15,128,256]{2,1,0:T(8,128)(2,1)S(1)} %shard_map.93.wide), custom_call_target="tpu_custom_call" | custom-call | tf_op jit(solution)/shard_map/pallas_call | solution.py:310
  38.7 8.2 %all-to-all-start.1 = ((bf16[8,32,128]{2,1,0:T(8,128)(2,1)}), bf16[8,32,128]{2,1,0:T(8,128)(2,1)S(1)}, u32[]{:S(2)}, u32[]{:S(2)}) async-start(bf16[8,32,128]{2,1,0:T(8,128)(2,1)} %get-tuple-element.31), calls=%async_computation.1 | async-start | bytes 131072 | tf_op jit(solution)/shard_map/all_to_all | solution.py:329
  46.9 0.0 copy-start
  46.9 0.0 copy-start.1
  46.9 4.6 %shard_map.95 = (bf16[128,128]{1,0:T(8,128)(2,1)S(1)}, bf16[128,128]{1,0:T(8,128)(2,1)S(1)}, bf16[3,128,256]{2,1,0:T(8,128)(2,1)S(1)}, bf16[3,128,256]{2,1,0:T(8...) custom-call(bf16[255,64,128]{2,1,0:T(8,128)(2,1)} %bitcast.6, ...), custom_call_target="tpu_custom_call" | custom-call | tf_op jit(solution)/shard_map/pallas_call | solution.py:310
  51.5 0.0 collective-permute-done.3.passed
  51.5 0.0 copy-done
  51.5 0.0 copy-done.1
  51.5 2.6 %shard_map.97 = (f32[8,64,256]{2,1,0:T(8,128)S(1)}, f32[8,64,64]{2,1,0:T(8,128)S(1)}, f32[32,128]{1,0:T(8,128)S(1)}) custom-call(s32[4,8]{1,0:T(4,128)S(1)} %bitcast.4, s32[8,8]{1,0:T(8,128)S(1)} %copy-done, bf16[2,10,64,256]{3,2,1,0:T(8,128)(2,1)S(1)} %shard_map.96.pair, bf16[2,10,64,256]{3,2,1,0:T(8,128)(2,1)S(1)} %collective-permute-done.2.moved, ...), custom_call_target="tpu_custom_call" | custom-call | tf_op jit(solution)/shard_map/pallas_call | solution.py:310
  54.1 0.1 all-to-all-done.1.received
  54.2 2.0 %shard_map.98 = bf16[8,64,256]{2,1,0:T(8,128)(2,1)} custom-call(bf16[8,32,128]{2,1,0:T(8,128)(2,1)S(1)} %all-to-all-done.1.received, bf16[128,128]{1,0:T(8,128)(2,1)S(1)} %get-tuple-element.32.next_high, bf16[128,128]{1,0:T(8,128)(2,1)S(1)} %get-tuple-element.33.next_low, bf16[3,128,256]{2,1,0:T(8,128)(2,1)S(1)} %get-tuple-element.34.cross_high, ...), custom_call_target="tpu_custom_call" | custom-call | tf_op jit(solution)/shard_map/pallas_call | solution.py:310
Async XLA Ops:
  2.1 4.5 %collective-permute-start.1 = (bf16[10,64,256]{2,1,0:T(8,128)(2,1)S(1)}, bf16[10,64,256]{2,1,0:T(8,128)(2,1)S(1)}, u32[]{:S(2)}, u32[]{:S(2)}) collective-permute-start(bf16[10,64,256]{2,1,0:T(8,128)(2,1)S(1)} %get-tuple-element.38.halo), channel_id=1, source_target_pairs={{0,1},{1,0},{2,3},{3,2},{4,5},{5,4},{6,7},{7,6},{8,9},{9,8},{10,11... | collective-permute-start | bytes 983048 | tf_op jit(solution)/shard_map/ppermute | solution.py:333
  6.8 11.3 %collective-permute-start.2 = (bf16[2,10,64,256]{3,2,1,0:T(8,128)(2,1)S(1)}, bf16[2,10,64,256]{3,2,1,0:T(8,128)(2,1)S(1)}, u32[]{:S(2)}, u32[]{:S(2)}) collective-permute-start(bf16[2,10,64,256]{3,2,1,0:T(8,128)(2,1)S(1)} %shard_map.96.pair), channel_id=1, source_target_pairs={{0,2},{2,4},{3,1},{4,6},{5,3},{6,8},{7,5},{8,10},{9,7},{10,12},{11... | collective-permute-start | bytes 1966088 | tf_op jit(solution)/shard_map/ppermute | solution.py:339
  18.9 32.5 %collective-permute-start.3 = (bf16[1,10,64,256]{3,2,1,0:T(8,128)(2,1)}, bf16[1,10,64,256]{3,2,1,0:T(8,128)(2,1)S(1)}, u32[]{:S(2)}, u32[]{:S(2)}) collective-permute-start(bf16[1,10,64,256]{3,2,1,0:T(8,128)(2,1)} %constant_dynamic-slice_fusion), channel_id=1, source_target_pairs={{0,1},{1,0},{2,3},{3,2},{4,5},{5,4},{6,7},{7,6},{8,9},{9,8},{10,11... | collective-permute-start | bytes 983048 | tf_op jit(solution)/shard_map/ppermute | solution.py:333
  18.9 1.9 %collective-permute-start = (f32[64,64]{1,0:T(8,128)S(1)}, f32[64,64]{1,0:T(8,128)S(1)}, u32[]{:S(2)}, u32[]{:S(2)}) collective-permute-start(f32[64,64]{1,0:T(8,128)S(1)} %get-tuple-element.27.root), channel_id=1, source_target_pairs={{0,1},{1,0},{2,3},{3,2},{4,5},{5,4},{6,7},{7,6},{8,9},{9,8},{10,11... | collective-permute-start | bytes 49160 | tf_op jit(solution)/shard_map/ppermute | solution.py:333
  21.7 15.7 %all-to-all-start = ((bf16[16,32,128]{2,1,0:T(8,128)(2,1)}), bf16[16,32,128]{2,1,0:T(8,128)(2,1)S(1)}, u32[]{:S(2)}, u32[]{:S(2)}) async-start(bf16[16,32,128]{2,1,0:T(8,128)(2,1)} %get-tuple-element.29), calls=%async_computation | async-start | bytes 262144 | tf_op jit(solution)/shard_map/all_to_all | solution.py:329
  38.7 15.5 %all-to-all-start.1 = ((bf16[8,32,128]{2,1,0:T(8,128)(2,1)}), bf16[8,32,128]{2,1,0:T(8,128)(2,1)S(1)}, u32[]{:S(2)}, u32[]{:S(2)}) async-start(bf16[8,32,128]{2,1,0:T(8,128)(2,1)} %get-tuple-element.31), calls=%async_computation.1 | async-start | bytes 131072 | tf_op jit(solution)/shard_map/all_to_all | solution.py:329
  46.9 4.6 %copy-start = (s32[8,8]{1,0:T(8,128)S(1)}, s32[8,8]{1,0:T(8,128)}, u32[]{:S(2)}) copy-start(s32[8,8]{1,0:T(8,128)} %far_ids.1) | copy-start | bytes 772
  46.9 4.6 %copy-start.1 = (s32[8,4]{0,1:T(4,128)S(1)}, s32[8,4]{0,1:T(4,128)}, u32[]{:S(2)}) copy-start(s32[8,4]{0,1:T(4,128)} %param.12) | copy-start | bytes 388
